TPU v7x, 512 devices: a whole 4x8x8 slice. The times are simulated.
512 devices in a mesh: node: 64 (over y, z), col: 8 (over x, core).
Axes of the slice: x: 4, y: 8, z: 8, core: 2. Of those that a mesh axis runs over, the one named last changes fastest.
Arguments:
- x_t: bfloat16 [512, 32768], P('col', 'node'), may hold values from -6 to 6
- adj_tiles: bfloat16 [4096, 128, 128], P('node'), may hold values from -0.1875 to 0.1875
- tile_rows: int32 [4096], P('node'), may hold values from 0 to 3
- tile_cols: int32 [4096], P('node'), may hold values from 0 to 255, as said below
- tile_counts: int32 [64], P('node'), may hold values from 8 to 64, as said below
- w_first: bfloat16 [512, 512], P('col'), may hold values from -0.25 to 0.25
- b_first: float32 [512], P('col'), may hold values from -3 to 3
- w_second: bfloat16 [512, 512], P('col'), may hold values from -0.25 to 0.25
- b_second: float32 [512], P('col'), may hold values from -3 to 3
Outputs:
- out_t: float32 [512, 32768], P('col', 'node')
Inputs may be any that keep to these rules, and one draw needn't show every extreme that they name: `tile_cols`: column blocks q * 4 to q * 4 + 3 belong to device q of node. Among the live tiles of one device, at most 2 distinct column blocks belong to any one device, and every device's first 2 tiles name 2 distinct blocks of one device. `tile_counts`: some device has all 64 slots live.
All inputs are finite; a program needn't handle non-finite values.
Results may differ from a plain program's by a relative error of at most 0.004.
Values may be sent and summed in bfloat16 or wider, within the bound.
A program may use at most 64 MiB of HBM per device.

v0:
```python
import jax
import jax.numpy as jnp
from jax import lax
from jax.sharding import PartitionSpec as P

BLK = 128
CAP = 2


def tile_sum(x_blocks, tile_values, selector):
    products = jnp.einsum("fnj,nij->fni", x_blocks, tile_values, preferred_element_type=jnp.float32)
    return jnp.einsum("fni,nb->fbi", products, selector, precision=lax.Precision.HIGHEST)


def aggregate(feat_t, adj_tiles, tile_rows, live_count, plan):
    feat_local = feat_t.shape[0]
    row_blocks = feat_t.shape[1] // BLK
    tile_total = adj_tiles.shape[0]
    asked_of, tile_slot = plan
    own_blocks = feat_t.reshape(feat_local, row_blocks, BLK)
    outgoing = jnp.take(own_blocks, asked_of.reshape(-1), axis=1)
    incoming = lax.all_to_all(outgoing, "node", split_axis=1, concat_axis=1, tiled=True)
    x_blocks = jnp.take(incoming, tile_slot, axis=1)
    is_live = jnp.arange(tile_total, dtype=jnp.int32) < live_count
    selector = (
        (tile_rows[:, None] == jnp.arange(row_blocks, dtype=jnp.int32)[None, :]) & is_live[:, None]
    ).astype(jnp.float32)
    summed = tile_sum(x_blocks, adj_tiles, selector)
    return summed.reshape(feat_local, row_blocks * BLK).astype(jnp.bfloat16)


def dense_layer(aggregated, weight_local, bias_local):
    summed = jnp.dot(
        weight_local,
        lax.all_gather(aggregated, "col", axis=0, tiled=True),
        preferred_element_type=jnp.float32,
    )
    return summed + bias_local[:, None]


def body(x_t, adj_tiles, tile_rows, tile_cols, tile_counts, w_first, b_first, w_second, b_second):
    row_blocks = x_t.shape[1] // BLK
    peer_count = lax.axis_size("node")
    block_total = peer_count * row_blocks
    live_count = tile_counts[0]
    is_live = jnp.arange(tile_cols.shape[0], dtype=jnp.int32) < live_count
    named = (tile_cols[:, None] == jnp.arange(block_total, dtype=jnp.int32)[None, :]) & is_live[
        :, None
    ]
    needed = jnp.any(named, axis=0).astype(jnp.int32).reshape(peer_count, row_blocks)
    position = jnp.cumsum(needed, axis=1) - 1
    slot_hit = (needed[:, :, None] == 1) & (
        position[:, :, None] == jnp.arange(CAP, dtype=jnp.int32)[None, None, :]
    )
    wanted = jnp.sum(
        slot_hit.astype(jnp.int32) * jnp.arange(row_blocks, dtype=jnp.int32)[None, :, None], axis=1
    )
    asked_of = lax.all_to_all(wanted, "node", split_axis=0, concat_axis=0, tiled=True)
    owner_base = (jnp.arange(peer_count, dtype=jnp.int32) * CAP)[:, None]
    slot_table = (owner_base + jnp.clip(position, 0, CAP - 1)).reshape(-1)
    tile_slot = jnp.take(slot_table, tile_cols)
    plan = (asked_of, tile_slot)
    y_first = aggregate(x_t, adj_tiles, tile_rows, live_count, plan)
    h_first = jnp.maximum(dense_layer(y_first, w_first, b_first), 0.0).astype(jnp.bfloat16)
    y_second = aggregate(h_first, adj_tiles, tile_rows, live_count, plan)
    return dense_layer(y_second, w_second, b_second)


def solution(mesh):
    return jax.shard_map(
        body,
        mesh=mesh,
        in_specs=(
            P("col", "node"),
            P("node", None, None),
            P("node"),
            P("node"),
            P("node"),
            P("col", None),
            P("col"),
            P("col", None),
            P("col"),
        ),
        out_specs=P("col", "node"),
        check_vma=False,
    )
```

profile of v0, /device:TPU:25, one launch (start us, length us, event | category | flops | bytes accessed | tf_op | source)
XLA Modules:
  0.0 206.9 jit_solution(1067784979185888805)
XLA Ops:
  0.0 0.0 copy-start
  0.8 0.8 fusion.23
  1.6 0.1 reshape.72
  1.7 0.1 copy.23
  1.8 0.2 reduce_window_sum.11
  2.0 0.1 clamp_add_fusion
  2.1 0.1 copy.24
  2.2 0.7 copy.25
  2.9 15.8 %all-to-all-start = ((s32[64,1,2]{2,1,0:T(1,128)}), s32[64,1,2]{2,1,0:T(1,128)S(1)}, u32[]{:S(2)}, u32[]{:S(2)}) async-start(s32[64,1,2]{2,1,0:T(1,128)} %copy.25), calls=%async_computation | async-start | bytes 65536 | tf_op jit(solution)/shard_map/all_to_all | solution.py:58
  18.7 0.9 copy_bitcast_fusion.3
  19.6 7.5 %all-to-all-done = s32[64,1,2]{2,1,0:T(1,128)S(1)} async-done(((s32[64,1,2]{2,1,0:T(1,128)}), s32[64,1,2]{2,1,0:T(1,128)S(1)}, u32[]{:S(2)}, u32[]{:S(2)}) %all-to-all-start) | async-done | bytes 544 | tf_op jit(solution)/shard_map/all_to_all | solution.py:58
  27.1 0.5 broadcast.114
  27.6 0.7 reduce.3
  28.3 0.1 reshape.70
  28.5 2.1 %gather_fusion.1 = bf16[128,64,128]{2,1,0:T(8,128)(2,1)} fusion(bf16[64,4,128]{2,0,1:T(8,128)(2,1)S(1)} %copy_bitcast_fusion.3, s32[1024]{0:T(1024)S(1)} %pad_clamp_fusion.1), kind=kCustom, calls=%fused_computation.clone | custom fusion | bytes 4194816 | tf_op jit(solution)/shard_map/jit(_take)/gather | solution.py:21
  30.6 3.2 %select_bitcast_fusion.1 = bf16[64,128,128]{2,0,1:T(8,128)(2,1)} fusion(bf16[128,64,128]{2,1,0:T(8,128)(2,1)} %gather_fusion.1, pred[128]{0:T(512)(128)(4,1)S(1)} %compare_and_fusion.1), kind=kLoop, calls=%fused_computation.10 | loop fusion | flops 1048576 | bytes 4194432 | tf_op jit(solution)/shard_map/jit(_take)/select_n | solution.py:21
  33.8 0.0 copy-start.5
  33.8 8.0 %all-to-all-start.1 = ((bf16[64,128,128]{2,0,1:T(8,128)(2,1)}), bf16[64,128,128]{2,0,1:T(8,128)(2,1)}, u32[]{:S(2)}, u32[]{:S(2)}) async-start(bf16[64,128,128]{2,0,1:T(8,128)(2,1)} %select_bitcast_fusion.1), calls=%async_computation.1 | async-start | bytes 4194304 | tf_op jit(solution)/shard_map/all_to_all | solution.py:22
  41.8 0.1 add.63
  41.9 0.0 copy-done.5
  42.0 0.8 gather_fusion
  42.8 53.7 %all-to-all-done.1 = bf16[64,128,128]{2,0,1:T(8,128)(2,1)} async-done(((bf16[64,128,128]{2,0,1:T(8,128)(2,1)}), bf16[64,128,128]{2,0,1:T(8,128)(2,1)}, u32[]{:S(2)}, u32[]{:S(2)}) %all-to-all-start.1) | async-done | bytes 2097184 | tf_op jit(solution)/shard_map/all_to_all | solution.py:22
  96.5 2.3 %gather_fusion.2 = bf16[64,64,128]{2,1,0:T(8,128)(2,1)S(1)} fusion(bf16[64,128,128]{2,0,1:T(8,128)(2,1)} %all-to-all-done.1, s32[1024]{0:T(1024)S(1)} %pad_clamp_fusion), kind=kCustom, calls=%fused_computation.1.clone | custom fusion | bytes 2097408 | tf_op jit(solution)/shard_map/jit(_take)/gather | solution.py:23
  98.8 0.0 copy-done
  98.8 0.0 copy-start.3
  98.8 1.5 convolution_bitcast_fusion.1
  100.4 0.0 copy-done.3
  100.4 0.0 copy-start.1
  100.4 0.0 copy-start.6
  100.4 2.0 fusion.7
  102.4 15.1 %all_gather.6 = bf16[512,512]{1,0:T(8,128)(2,1)S(1)} all-gather(bf16[64,512]{1,0:T(8,128)(2,1)S(1)} %bitcast.53), channel_id=1, replica_groups=mesh['node'=64,'col'=8] {'col'}, dimensions={0}, use_global_device_ids=true | all-gather | bytes 589824 | tf_op jit(solution)/shard_map/all_gather | solution.py:35
  117.5 0.0 copy-done.1
  117.5 0.0 copy-done.6
  117.5 0.2 fusion.13
  117.7 2.2 %gather_fusion.3 = bf16[128,64,128]{2,1,0:T(8,128)(2,1)} fusion(bf16[64,4,128]{2,0,1:T(8,128)(2,1)S(1)} %bitcast.50, s32[1024]{0:T(1024)S(1)} %pad_clamp_fusion.1), kind=kCustom, calls=%fused_computation.2.clone | custom fusion | bytes 4194816 | tf_op jit(solution)/shard_map/jit(_take)/gather | solution.py:21
  119.9 1.9 select_bitcast_fusion
  121.7 62.4 %all_to_all.19 = bf16[64,128,128]{2,0,1:T(8,128)(2,1)} all-to-all(bf16[64,128,128]{2,0,1:T(8,128)(2,1)S(1)} %select_bitcast_fusion), channel_id=1, replica_groups=mesh['node'=64,'col'=8] {'node'}, dimensions={1} | all-to-all | bytes 4194304 | tf_op jit(solution)/shard_map/all_to_all | solution.py:22
  184.1 2.3 %gather_fusion.4 = bf16[64,64,128]{2,1,0:T(8,128)(2,1)S(1)} fusion(bf16[64,128,128]{2,0,1:T(8,128)(2,1)} %all_to_all.19, s32[1024]{0:T(1024)S(1)} %pad_clamp_fusion), kind=kCustom, calls=%fused_computation.3.clone | custom fusion | bytes 2097408 | tf_op jit(solution)/shard_map/jit(_take)/gather | solution.py:23
  186.4 1.5 convolution_bitcast_fusion
  188.0 0.0 copy-start.2
  188.0 0.0 copy-start.4
  188.0 2.0 fusion.10
  190.0 16.0 %all_gather.7 = bf16[512,512]{1,0:T(8,128)(2,1)S(1)} all-gather(bf16[64,512]{1,0:T(8,128)(2,1)S(1)} %bitcast.54), channel_id=1, replica_groups=mesh['node'=64,'col'=8] {'col'}, dimensions={0}, use_global_device_ids=true | all-gather | bytes 589824 | tf_op jit(solution)/shard_map/all_gather | solution.py:35
  206.0 0.0 copy-done.2
  206.0 0.0 copy-done.4
  206.0 0.9 fusion.4
  (15 shorter events, 0.1 us)
Async XLA Ops:
  0.0 98.8 %copy-start = (bf16[64,128,128]{2,1,0:T(8,128)(2,1)S(1)}, bf16[64,128,128]{2,1,0:T(8,128)(2,1)}, u32[]{:S(2)}) copy-start(bf16[64,128,128]{2,1,0:T(8,128)(2,1)} %param.14) | copy-start | bytes 6291460
  2.9 24.2 %all-to-all-start = ((s32[64,1,2]{2,1,0:T(1,128)}), s32[64,1,2]{2,1,0:T(1,128)S(1)}, u32[]{:S(2)}, u32[]{:S(2)}) async-start(s32[64,1,2]{2,1,0:T(1,128)} %copy.25), calls=%async_computation | async-start | bytes 65536 | tf_op jit(solution)/shard_map/all_to_all | solution.py:58
  33.8 8.1 %copy-start.5 = (s32[64]{0:T(128)S(1)}, s32[64]{0:T(128)}, u32[]{:S(2)}) copy-start(s32[64]{0:T(128)} %param.16) | copy-start | bytes 772
  33.8 62.7 %all-to-all-start.1 = ((bf16[64,128,128]{2,0,1:T(8,128)(2,1)}), bf16[64,128,128]{2,0,1:T(8,128)(2,1)}, u32[]{:S(2)}, u32[]{:S(2)}) async-start(bf16[64,128,128]{2,0,1:T(8,128)(2,1)} %select_bitcast_fusion.1), calls=%async_computation.1 | async-start | bytes 4194304 | tf_op jit(solution)/shard_map/all_to_all | solution.py:22
  98.8 1.6 copy-start.3
  100.4 17.1 %copy-start.1 = (bf16[64,512]{1,0:T(8,128)(2,1)S(1)}, bf16[64,512]{1,0:T(8,128)(2,1)}, u32[]{:S(2)}) copy-start(bf16[64,512]{1,0:T(8,128)(2,1)} %param.18) | copy-start | bytes 196612
  100.4 17.1 %copy-start.6 = (f32[64]{0:T(128)S(1)}, f32[64]{0:T(128)}, u32[]{:S(2)}) copy-start(f32[64]{0:T(128)} %param.19) | copy-start | bytes 772
  188.0 18.1 %copy-start.2 = (bf16[64,512]{1,0:T(8,128)(2,1)S(1)}, bf16[64,512]{1,0:T(8,128)(2,1)}, u32[]{:S(2)}) copy-start(bf16[64,512]{1,0:T(8,128)(2,1)} %param.20) | copy-start | bytes 196612
  188.0 18.0 %copy-start.4 = (f32[64]{0:T(128)S(1)}, f32[64]{0:T(128)}, u32[]{:S(2)}) copy-start(f32[64]{0:T(128)} %param.21) | copy-start | bytes 772
where the time goes:
time: 207 us
  blocking collectives  93.5 us (45%)
  waiting for transfers between devices  61.2 us (30%)
  starting transfers between devices  23.9 us (12%)
  local copies, waits for them, and re-layouts  12.4 us (6%)
  matrix products  8.07 us (4%)
  other arithmetic  6.84 us (3%)
    all_to_all x1, blocking collectives, aggregate(): lax.all_to_all(outgoing, 'node', split_axis=1, concat_axis=1, tiled=True)  62.4 us
    all_to_all x1, waiting for transfers between devices, aggregate(): lax.all_to_all(outgoing, 'node', split_axis=1, concat_axis=1, tiled=True)  53.7 us
    all_gather x2, blocking collectives, dense_layer(): lax.all_gather(aggregated, 'col', axis=0, tiled=True)  31.1 us
    all_to_all x1, starting transfers between devices, body(): lax.all_to_all(wanted, 'node', split_axis=0, concat_axis=0, tiled=True)  15.8 us
    all_to_all x1, starting transfers between devices, aggregate(): lax.all_to_all(outgoing, 'node', split_axis=1, concat_axis=1, tiled=True)  8.02 us
    all_to_all x1, waiting for transfers between devices, body(): lax.all_to_all(wanted, 'node', split_axis=0, concat_axis=0, tiled=True)  7.51 us
    select_n x3, other arithmetic, aggregate(): outgoing = jnp.take(own_blocks, asked_of.reshape(-1), axis=1)  5.01 us
    gather x2, local copies, waits for them, and re-layouts, aggregate(): x_blocks = jnp.take(incoming, tile_slot, axis=1)  4.68 us
  transfers between devices with their start and end apart: 2, of which 2 were waited for; matrix products, arithmetic and copies ran while one was open for 1% of the time, Pallas kernels for 0%

commit v1 on v0

--- a/solution.py
+++ b/solution.py
@@ -1,10 +1,23 @@
+import functools
 import jax
 import jax.numpy as jnp
 from jax import lax
 from jax.sharding import PartitionSpec as P
+from jax.lax import all_to_all, psum
 
 BLK = 128
 CAP = 2
+
+
+def apply_positions_by_axis(field_in, a_name):
+    y1 = psum(1, axis_name=a_name)
+    clean = jnp.split(field_in, y1, axis=1)
+    ready = jnp.stack(clean, axis=0)
+    block_next = all_to_all(ready, concat_axis=0, split_axis=0, axis_name=a_name)
+    return jnp.concatenate(block_next, axis=1)
+
+
+cover_series_all = functools.partial(apply_positions_by_axis, a_name="node")
 
 
 def tile_sum(x_blocks, tile_values, selector):
@@ -19,7 +32,7 @@
     asked_of, tile_slot = plan
     own_blocks = feat_t.reshape(feat_local, row_blocks, BLK)
     outgoing = jnp.take(own_blocks, asked_of.reshape(-1), axis=1)
-    incoming = lax.all_to_all(outgoing, "node", split_axis=1, concat_axis=1, tiled=True)
+    incoming = cover_series_all(outgoing)
     x_blocks = jnp.take(incoming, tile_slot, axis=1)
     is_live = jnp.arange(tile_total, dtype=jnp.int32) < live_count
     selector = (

time: 207 us -> 246 us (1.19)
  local copies, waits for them, and re-layouts: 12.4 us -> 52.4 us
    unnamed x16 -> x142, local copies, waits for them, and re-layouts: 0.06 us -> 39.3 us
where the time goes in v1:
time: 246 us
  blocking collectives  93.4 us (38%)
  waiting for transfers between devices  60.6 us (25%)
  local copies, waits for them, and re-layouts  52.4 us (21%)
  starting transfers between devices  23.9 us (10%)
  matrix products  8.07 us (3%)
  other arithmetic  6.18 us (3%)
    all_to_all x1, blocking collectives, apply_positions_by_axis(): all_to_all(ready, concat_axis=0, split_axis=0, axis_name=a_name)  62.2 us
    all_to_all x1, waiting for transfers between devices, apply_positions_by_axis(): all_to_all(ready, concat_axis=0, split_axis=0, axis_name=a_name)  53.7 us
    unnamed x142, local copies, waits for them, and re-layouts  39.3 us
    all_gather x2, blocking collectives, dense_layer(): lax.all_gather(aggregated, 'col', axis=0, tiled=True)  31.3 us
    all_to_all x1, starting transfers between devices, body(): lax.all_to_all(wanted, 'node', split_axis=0, concat_axis=0, tiled=True)  15.8 us
    all_to_all x1, starting transfers between devices, apply_positions_by_axis(): all_to_all(ready, concat_axis=0, split_axis=0, axis_name=a_name)  8.02 us
    all_to_all x1, waiting for transfers between devices, body(): lax.all_to_all(wanted, 'node', split_axis=0, concat_axis=0, tiled=True)  6.85 us
  transfers between devices with their start and end apart: 2, of which 2 were waited for; matrix products, arithmetic and copies ran while one was open for 1% of the time, Pallas kernels for 0%

profile of v1, /device:TPU:25, one launch (start us, length us, event | category | flops | bytes accessed | tf_op | source)
XLA Modules:
  0.0 245.8 jit_solution(7650705404028262723)
XLA Ops:
  0.8 0.8 fusion.23
  2.2 0.7 copy.25
  2.9 15.8 %all-to-all-start = ((s32[64,1,2]{2,1,0:T(1,128)}), s32[64,1,2]{2,1,0:T(1,128)S(1)}, u32[]{:S(2)}, u32[]{:S(2)}) async-start(s32[64,1,2]{2,1,0:T(1,128)} %copy.25), calls=%async_computation | async-start | bytes 65536 | tf_op jit(solution)/shard_map/all_to_all | solution.py:71
  18.7 0.9 copy_bitcast_fusion.3
  19.6 0.7 compare_select_fusion.2
  20.2 6.9 %all-to-all-done = s32[64,1,2]{2,1,0:T(1,128)S(1)} async-done(((s32[64,1,2]{2,1,0:T(1,128)}), s32[64,1,2]{2,1,0:T(1,128)S(1)}, u32[]{:S(2)}, u32[]{:S(2)}) %all-to-all-start) | async-done | bytes 544 | tf_op jit(solution)/shard_map/all_to_all | solution.py:71
  27.6 0.7 reduce.3
  28.5 2.2 gather_fusion.1
  30.7 1.9 select_bitcast_fusion.1
  32.5 0.6 constant_dynamic-update-slice_fusion.63
  33.1 0.6 constant_dynamic-update-slice_fusion.62
  33.8 0.6 constant_dynamic-update-slice_fusion.61
  34.4 0.6 constant_dynamic-update-slice_fusion.60
  35.0 0.6 constant_dynamic-update-slice_fusion.59
  35.6 0.6 constant_dynamic-update-slice_fusion.58
  36.2 0.6 constant_dynamic-update-slice_fusion.57
  38.1 0.6 constant_dynamic-update-slice_fusion.54
  38.7 0.6 constant_dynamic-update-slice_fusion.53
  39.9 0.6 constant_dynamic-update-slice_fusion.51
  40.5 0.6 constant_dynamic-update-slice_fusion.50
  41.7 0.6 constant_dynamic-update-slice_fusion.48
  43.0 0.6 constant_dynamic-update-slice_fusion.46
  43.6 0.6 constant_dynamic-update-slice_fusion.45
  44.2 0.6 constant_dynamic-update-slice_fusion.44
  44.8 0.6 constant_dynamic-update-slice_fusion.43
  45.4 0.6 constant_dynamic-update-slice_fusion.42
  46.0 0.6 constant_dynamic-update-slice_fusion.41
  46.7 0.6 constant_dynamic-update-slice_fusion.40
  49.1 0.6 constant_dynamic-update-slice_fusion.36
  49.7 0.6 constant_dynamic-update-slice_fusion.35
  50.9 0.6 constant_dynamic-update-slice_fusion.33
  52.2 0.6 constant_dynamic-update-slice_fusion.31
  52.8 0.6 constant_dynamic-update-slice_fusion.30
  54.0 0.6 constant_dynamic-update-slice_fusion.28
  54.6 0.6 constant_dynamic-update-slice_fusion.27
  57.0 0.6 constant_dynamic-update-slice_fusion.23
  57.7 0.6 constant_dynamic-update-slice_fusion.22
  58.9 0.6 constant_dynamic-update-slice_fusion.20
  59.5 0.6 constant_dynamic-update-slice_fusion.19
  61.3 0.6 constant_dynamic-update-slice_fusion.16
  62.0 0.6 constant_dynamic-update-slice_fusion.15
  63.2 0.6 constant_dynamic-update-slice_fusion.13
  63.8 0.6 constant_dynamic-update-slice_fusion.12
  66.2 0.6 constant_dynamic-update-slice_fusion.8
  66.9 0.6 constant_dynamic-update-slice_fusion.7
  67.5 0.6 constant_dynamic-update-slice_fusion.6
  68.1 0.6 constant_dynamic-update-slice_fusion.5
  68.7 0.6 constant_dynamic-update-slice_fusion.4
  71.1 0.6 constant_dynamic-update-slice_fusion
  71.8 8.0 %all-to-all-start.1 = ((bf16[64,64,2,128]{3,1,2,0:T(8,128)(2,1)}), bf16[64,64,2,128]{3,1,2,0:T(8,128)(2,1)}, u32[]{:S(2)}, u32[]{:S(2)}) async-start(bf16[64,64,2,128]{3,1,2,0:T(8,128)(2,1)} %constant_dynamic-update-slice_fusion), calls=%async_computation.1 | async-start | bytes 4194304 | tf_op jit(solution)/shard_map/all_to_all | solution.py:16
  79.9 0.8 gather_fusion
  80.7 53.7 %all-to-all-done.1 = bf16[64,64,2,128]{3,1,2,0:T(8,128)(2,1)} async-done(((bf16[64,64,2,128]{3,1,2,0:T(8,128)(2,1)}), bf16[64,64,2,128]{3,1,2,0:T(8,128)(2,1)}, u32[]{:S(2)}, u32[]{:S(2)}) %all-to-all-start.1) | async-done | bytes 2097184 | tf_op jit(solution)/shard_map/all_to_all | solution.py:16
  134.5 2.3 gather_fusion.2
  136.8 1.5 convolution_bitcast_fusion.1
  138.4 2.0 fusion.7
  140.4 15.1 %all_gather.6 = bf16[512,512]{1,0:T(8,128)(2,1)S(1)} all-gather(bf16[64,512]{1,0:T(8,128)(2,1)S(1)} %bitcast.572), channel_id=1, replica_groups=mesh['node'=64,'col'=8] {'col'}, dimensions={0}, use_global_device_ids=true | all-gather | bytes 589824 | tf_op jit(solution)/shard_map/all_gather | solution.py:48
  155.7 2.2 gather_fusion.3
  157.9 1.9 select_bitcast_fusion
  160.7 62.2 %all_to_all.19 = bf16[64,64,2,128]{3,1,2,0:T(8,128)(2,1)} all-to-all(bf16[64,64,2,128]{3,1,2,0:T(8,128)(2,1)S(1)} %constant_dynamic-update-slice_fusion.64), channel_id=1, replica_groups=mesh['node'=64,'col'=8] {'node'}, dimensions={0} | all-to-all | bytes 4194304 | tf_op jit(solution)/shard_map/all_to_all | solution.py:16
  222.9 2.3 gather_fusion.4
  225.2 1.5 convolution_bitcast_fusion
  226.8 2.0 fusion.10
  228.8 16.2 %all_gather.7 = bf16[512,512]{1,0:T(8,128)(2,1)S(1)} all-gather(bf16[64,512]{1,0:T(8,128)(2,1)S(1)} %bitcast.573), channel_id=1, replica_groups=mesh['node'=64,'col'=8] {'col'}, dimensions={0}, use_global_device_ids=true | all-gather | bytes 589824 | tf_op jit(solution)/shard_map/all_gather | solution.py:48
  245.0 0.9 fusion.4
  (124 shorter events, 16.9 us)
Async XLA Ops:
  0.0 136.8 %copy-start = (bf16[64,128,128]{2,1,0:T(8,128)(2,1)S(1)}, bf16[64,128,128]{2,1,0:T(8,128)(2,1)}, u32[]{:S(2)}) copy-start(bf16[64,128,128]{2,1,0:T(8,128)(2,1)} %param.14) | copy-start | bytes 6291460
  2.9 24.2 %all-to-all-start = ((s32[64,1,2]{2,1,0:T(1,128)}), s32[64,1,2]{2,1,0:T(1,128)S(1)}, u32[]{:S(2)}, u32[]{:S(2)}) async-start(s32[64,1,2]{2,1,0:T(1,128)} %copy.25), calls=%async_computation | async-start | bytes 65536 | tf_op jit(solution)/shard_map/all_to_all | solution.py:71
  71.8 8.9 %copy-start.5 = (s32[64]{0:T(128)S(1)}, s32[64]{0:T(128)}, u32[]{:S(2)}) copy-start(s32[64]{0:T(128)} %param.16) | copy-start | bytes 772
  71.8 62.7 %all-to-all-start.1 = ((bf16[64,64,2,128]{3,1,2,0:T(8,128)(2,1)}), bf16[64,64,2,128]{3,1,2,0:T(8,128)(2,1)}, u32[]{:S(2)}, u32[]{:S(2)}) async-start(bf16[64,64,2,128]{3,1,2,0:T(8,128)(2,1)} %constant_dynamic-update-slice_fusion), calls=%async_computation.1 | async-start | bytes 4194304 | tf_op jit(solution)/shard_map/all_to_all | solution.py:16
  136.8 1.6 copy-start.3
  138.4 17.1 %copy-start.1 = (bf16[64,512]{1,0:T(8,128)(2,1)S(1)}, bf16[64,512]{1,0:T(8,128)(2,1)}, u32[]{:S(2)}) copy-start(bf16[64,512]{1,0:T(8,128)(2,1)} %param.18) | copy-start | bytes 196612
  138.4 17.1 %copy-start.6 = (f32[64]{0:T(128)S(1)}, f32[64]{0:T(128)}, u32[]{:S(2)}) copy-start(f32[64]{0:T(128)} %param.19) | copy-start | bytes 772
  226.8 18.2 %copy-start.2 = (bf16[64,512]{1,0:T(8,128)(2,1)S(1)}, bf16[64,512]{1,0:T(8,128)(2,1)}, u32[]{:S(2)}) copy-start(bf16[64,512]{1,0:T(8,128)(2,1)} %param.20) | copy-start | bytes 196612
  226.8 18.2 %copy-start.4 = (f32[64]{0:T(128)S(1)}, f32[64]{0:T(128)}, u32[]{:S(2)}) copy-start(f32[64]{0:T(128)} %param.21) | copy-start | bytes 772
